TPU v7x, 128 devices: a whole 4x4x4 slice. The times are simulated.
128 devices in a mesh: row: 8 (over z, core), col: 16 (over y, x).
Axes of the slice: x: 4, y: 4, z: 4, core: 2. Of those that a mesh axis runs over, the one named last changes fastest.
Arguments:
- symmetric: float32 [16384, 16384], P('row', 'col'), may hold values from -8 to 8, as said below
- reflectors: float32 [4, 64, 16384], P(None, None, ('row', 'col')), may hold values from -0.125 to 0.125
- tri_factor: float32 [4, 64, 64], replicated, may hold values from -0.4 to 1.5, as said below
Outputs:
- updated: float32 [16384, 16384], P('row', 'col')
Inputs may be any that keep to these rules, and one draw needn't show every extreme that they name: symmetric is a symmetric matrix. Each tri_factor[p] is upper triangular.
All inputs are finite; a program needn't handle non-finite values.
Results may differ from a plain program's by a relative error of at most 0.00029.
Values sent between devices are 32-bit elements; how exact they have to be, the bound alone decides.
A program may use at most 64 MiB of HBM per device.

v0:
```python
import jax
import jax.numpy as jnp
from jax import lax
from jax.sharding import PartitionSpec as P


def broadcast(value, axis, source):
    kept = jnp.where(lax.axis_index(axis) == source, value, 0).astype(value.dtype)
    return lax.psum(kept, axis)


def shards(symmetric, reflectors, tri_factor):
    highest = lax.Precision.HIGHEST
    cols_here = symmetric.shape[1]
    row_count = lax.axis_size("row")
    col_count = lax.axis_size("col")
    col_index = lax.axis_index("col")
    owner = col_index * row_count // col_count
    offset = col_index % (col_count // row_count) * cols_here
    matrix = symmetric
    for panel in range(reflectors.shape[0]):
        piece = reflectors[panel]
        factor = tri_factor[panel]
        reflect_rows = lax.all_gather(piece, "col", axis=1, tiled=True)
        reflect_cols = broadcast(
            lax.dynamic_slice_in_dim(reflect_rows, offset, cols_here, 1), "row", owner
        )
        partial_value = lax.dot_general(
            reflect_cols,
            matrix,
            (((1,), (1,)), ((), ())),
            precision=highest,
            preferred_element_type=jnp.float32,
        )
        product_rows = lax.psum(partial_value, "col")
        image_rows = jnp.dot(
            factor.T, product_rows, precision=highest, preferred_element_type=jnp.float32
        )
        local_inner = lax.dot_general(
            reflect_rows,
            image_rows,
            (((1,), (1,)), ((), ())),
            precision=highest,
            preferred_element_type=jnp.float32,
        )
        inner = lax.psum(local_inner, "row")
        coupling = jnp.dot(factor.T, inner, precision=highest, preferred_element_type=jnp.float32)
        update_rows = image_rows - 0.5 * jnp.dot(
            coupling.T, reflect_rows, precision=highest, preferred_element_type=jnp.float32
        )
        update_cols = broadcast(
            lax.dynamic_slice_in_dim(update_rows, offset, cols_here, 1), "row", owner
        )
        left_block = jnp.concatenate([reflect_rows, update_rows], axis=0)
        right_block = jnp.concatenate([update_cols, reflect_cols], axis=0)
        matrix = matrix - lax.dot_general(
            left_block,
            right_block,
            (((0,), (0,)), ((), ())),
            precision=highest,
            preferred_element_type=jnp.float32,
        )
    return matrix


def solution(mesh):
    placed = (P("row", "col"), P(None, None, ("row", "col")), P())
    return jax.shard_map(
        shards, mesh=mesh, in_specs=placed, out_specs=P("row", "col"), check_vma=False
    )
```

profile of v0, /device:TPU:0, one launch (start us, length us, event | category | flops | bytes accessed | tf_op | source)
XLA Modules:
  0.0 878.7 jit_solution(7771888216284126579)
XLA Ops:
  6.5 0.9 fusion.64
  7.4 25.2 %all-gather = f32[1,64,2048]{2,1,0:T(8,128)S(1)} all-gather(f32[1,64,128]{2,1,0:T(8,128)S(1)} %get-tuple-element.13), channel_id=2, replica_groups=mesh['row'=8,'col'=16] {'col'}, dimensions={2}, use_global_device_ids=true | all-gather | bytes 557056 | tf_op jit(solution)/shard_map/all_gather | solution.py:24
  32.6 0.7 select_bitcast_fusion.3
  33.4 60.0 %all-reduce.13.cloned.1.call-done = f32[64,1024]{1,0:T(8,128)} async-done(((f32[64,1024]{1,0:T(8,128)}), f32[64,1024]{1,0:T(8,128)}) %all-reduce.13.cloned.1.call-update) | async-done | bytes 262160 | tf_op jit(solution)/shard_map/psum | solution.py:9
  93.4 12.3 %fusion.65 = f32[64,2048]{1,0:T(8,128)} fusion(f32[64,1024]{1,0:T(8,128)} %all-reduce.13.cloned.1.call-done, f32[2048,1024]{1,0:T(8,128)} %param.3), kind=kOutput, calls=%fused_computation.85 | convolution fusion | flops 1610612736 | bytes 9175040 | tf_op jit(solution)/shard_map/dot_general | solution.py:28
  105.7 25.3 %all-gather.1 = f32[1,64,2048]{2,1,0:T(8,128)S(1)} all-gather(f32[1,64,128]{2,1,0:T(8,128)S(1)} %get-tuple-element.12), channel_id=3, replica_groups=mesh['row'=8,'col'=16] {'col'}, dimensions={2}, use_global_device_ids=true | all-gather | bytes 557056 | tf_op jit(solution)/shard_map/all_gather | solution.py:24
  131.0 0.7 select_bitcast_fusion.2
  131.7 58.1 %all-reduce.15.cloned.1.call-done = f32[64,2048]{1,0:T(8,128)} async-done(((f32[64,2048]{1,0:T(8,128)}), f32[64,2048]{1,0:T(8,128)}) %all-reduce.15.cloned.1.call-update) | async-done | bytes 524304 | tf_op jit(solution)/shard_map/psum | solution.py:35
  189.9 1.7 fusion.42
  191.5 0.6 convolution_bitcast_fusion.3
  192.1 24.4 %psum.114 = f32[64,64]{0,1:T(8,128)S(1)} all-reduce(f32[64,64]{0,1:T(8,128)S(1)} %convolution_bitcast_fusion.3), channel_id=1, replica_groups=mesh['row'=8,'col'=16] {'row'}, use_global_device_ids=true, to_apply=%region_2.3 | all-reduce | flops 4096 | bytes 32768 | tf_op jit(solution)/shard_map/psum | solution.py:46
  216.7 0.6 fusion.3
  217.3 0.7 dynamic-slice_select_fusion.3
  218.3 57.3 %all-reduce.29.cloned.1.call-done = (f32[64,1024]{1,0:T(8,128)}, f32[64,1024]{1,0:T(8,128)}) async-done(((f32[64,1024]{1,0:T(8,128)}, f32[64,1024]{1,0:T(8,128)}), (f32[64,1024]{1,0:T(8,128)}, f32[64,1024]{1,0:T(8,128)})) %all-reduce.29.cloned.1.call-update) | async-done | bytes 524304 | tf_op jit(solution)/shard_map/psum | solution.py:9
  275.6 12.9 %convolution_subtract_fusion.3 = f32[2048,1024]{1,0:T(8,128)S(1)} fusion(f32[2048,1024]{1,0:T(8,128)} %param.3, f32[64,2048]{1,0:T(8,128)S(1)} %fusion.3, f32[64,2048]{1,0:T(8,128)S(1)} %bitcast.91, f32[64,1024]{1,0:T(8,128)S(1)} %copy-done.6, f32[64,1024]{1,0:T(8,128)} %get-tuple-element.9), kind=kOutput, calls=%fused_computation.3 | convolution fusion | flops 3223715840 | bytes 18350080 | tf_op jit(solution)/shard_map/dot_general | solution.py:56
  288.5 3.4 copy-done.1
  291.9 8.9 %fusion.66 = f32[64,2048]{1,0:T(8,128)} fusion(f32[64,1024]{1,0:T(8,128)S(1)} %copy-done.4, f32[2048,1024]{1,0:T(8,128)S(1)} %convolution_subtract_fusion.3), kind=kOutput, calls=%fused_computation.86 | convolution fusion | flops 1610612736 | bytes 9175040 | tf_op jit(solution)/shard_map/dot_general | solution.py:28
  300.8 25.4 %all-gather.2 = f32[1,64,2048]{2,1,0:T(8,128)S(1)} all-gather(f32[1,64,128]{2,1,0:T(8,128)S(1)} %get-tuple-element.14), channel_id=4, replica_groups=mesh['row'=8,'col'=16] {'col'}, dimensions={2}, use_global_device_ids=true | all-gather | bytes 557056 | tf_op jit(solution)/shard_map/all_gather | solution.py:24
  326.2 0.7 select_bitcast_fusion.1
  327.0 58.3 %all-reduce.17.cloned.1.call-done = f32[64,2048]{1,0:T(8,128)} async-done(((f32[64,2048]{1,0:T(8,128)}), f32[64,2048]{1,0:T(8,128)}) %all-reduce.17.cloned.1.call-update) | async-done | bytes 524304 | tf_op jit(solution)/shard_map/psum | solution.py:35
  385.2 1.7 fusion.38
  386.9 0.6 convolution_bitcast_fusion.2
  387.5 24.4 %psum.118 = f32[64,64]{0,1:T(8,128)S(1)} all-reduce(f32[64,64]{0,1:T(8,128)S(1)} %convolution_bitcast_fusion.2), channel_id=1, replica_groups=mesh['row'=8,'col'=16] {'row'}, use_global_device_ids=true, to_apply=%region_6.7 | all-reduce | flops 4096 | bytes 32768 | tf_op jit(solution)/shard_map/psum | solution.py:46
  412.1 0.6 fusion.2
  412.6 0.7 dynamic-slice_select_fusion.2
  413.8 57.1 %all-reduce.27.cloned.1.call-done = (f32[64,1024]{1,0:T(8,128)}, f32[64,1024]{1,0:T(8,128)}) async-done(((f32[64,1024]{1,0:T(8,128)}, f32[64,1024]{1,0:T(8,128)}), (f32[64,1024]{1,0:T(8,128)}, f32[64,1024]{1,0:T(8,128)})) %all-reduce.27.cloned.1.call-update) | async-done | bytes 524304 | tf_op jit(solution)/shard_map/psum | solution.py:9
  471.0 12.9 %convolution_subtract_fusion.2 = f32[2048,1024]{1,0:T(8,128)S(1)} fusion(f32[2048,1024]{1,0:T(8,128)} %copy-done.1, f32[64,2048]{1,0:T(8,128)S(1)} %fusion.2, f32[64,2048]{1,0:T(8,128)S(1)} %bitcast.89, f32[64,1024]{1,0:T(8,128)S(1)} %copy-done.4, f32[64,1024]{1,0:T(8,128)} %get-tuple-element.7), kind=kOutput, calls=%fused_computation.2 | convolution fusion | flops 3223715840 | bytes 18350080 | tf_op jit(solution)/shard_map/dot_general | solution.py:56
  483.9 3.4 copy-done
  487.3 8.9 %fusion.67 = f32[64,2048]{1,0:T(8,128)} fusion(f32[64,1024]{1,0:T(8,128)S(1)} %copy-done.3, f32[2048,1024]{1,0:T(8,128)S(1)} %convolution_subtract_fusion.2), kind=kOutput, calls=%fused_computation.87 | convolution fusion | flops 1610612736 | bytes 9175040 | tf_op jit(solution)/shard_map/dot_general | solution.py:28
  496.2 25.4 %all-gather.3 = f32[1,64,2048]{2,1,0:T(8,128)S(1)} all-gather(f32[1,64,128]{2,1,0:T(8,128)S(1)} %get-tuple-element.11), channel_id=5, replica_groups=mesh['row'=8,'col'=16] {'col'}, dimensions={2}, use_global_device_ids=true | all-gather | bytes 557056 | tf_op jit(solution)/shard_map/all_gather | solution.py:24
  521.6 0.7 select_bitcast_fusion
  522.4 58.3 %all-reduce.19.cloned.1.call-done = f32[64,2048]{1,0:T(8,128)} async-done(((f32[64,2048]{1,0:T(8,128)}), f32[64,2048]{1,0:T(8,128)}) %all-reduce.19.cloned.1.call-update) | async-done | bytes 524304 | tf_op jit(solution)/shard_map/psum | solution.py:35
  580.6 1.7 fusion.34
  582.3 0.6 convolution_bitcast_fusion.1
  582.9 24.4 %psum.122 = f32[64,64]{0,1:T(8,128)S(1)} all-reduce(f32[64,64]{0,1:T(8,128)S(1)} %convolution_bitcast_fusion.1), channel_id=1, replica_groups=mesh['row'=8,'col'=16] {'row'}, use_global_device_ids=true, to_apply=%region_10.11 | all-reduce | flops 4096 | bytes 32768 | tf_op jit(solution)/shard_map/psum | solution.py:46
  607.5 0.6 fusion.1
  608.1 0.7 dynamic-slice_select_fusion.1
  609.0 57.3 %all-reduce.25.cloned.1.call-done = (f32[64,1024]{1,0:T(8,128)}, f32[64,1024]{1,0:T(8,128)}) async-done(((f32[64,1024]{1,0:T(8,128)}, f32[64,1024]{1,0:T(8,128)}), (f32[64,1024]{1,0:T(8,128)}, f32[64,1024]{1,0:T(8,128)})) %all-reduce.25.cloned.1.call-update) | async-done | bytes 524304 | tf_op jit(solution)/shard_map/psum | solution.py:9
  666.3 12.9 %convolution_subtract_fusion.1 = f32[2048,1024]{1,0:T(8,128)S(1)} fusion(f32[2048,1024]{1,0:T(8,128)} %copy-done, f32[64,2048]{1,0:T(8,128)S(1)} %fusion.1, f32[64,2048]{1,0:T(8,128)S(1)} %bitcast.88, f32[64,1024]{1,0:T(8,128)S(1)} %copy-done.3, f32[64,1024]{1,0:T(8,128)} %get-tuple-element.5), kind=kOutput, calls=%fused_computation.1 | convolution fusion | flops 3223715840 | bytes 18350080 | tf_op jit(solution)/shard_map/dot_general | solution.py:56
  679.2 3.4 copy-done.2
  682.6 8.9 %fusion.68 = f32[64,2048]{1,0:T(8,128)} fusion(f32[64,1024]{1,0:T(8,128)S(1)} %copy-done.5, f32[2048,1024]{1,0:T(8,128)S(1)} %convolution_subtract_fusion.1), kind=kOutput, calls=%fused_computation.88 | convolution fusion | flops 1610612736 | bytes 9175040 | tf_op jit(solution)/shard_map/dot_general | solution.py:28
  691.6 84.2 %all-reduce.21.cloned.1.call-done = f32[64,2048]{1,0:T(8,128)} async-done(((f32[64,2048]{1,0:T(8,128)}), f32[64,2048]{1,0:T(8,128)}) %all-reduce.21.cloned.1.call-update) | async-done | bytes 524304 | tf_op jit(solution)/shard_map/psum | solution.py:35
  775.8 1.7 fusion.30
  778.1 24.8 %psum.126 = f32[64,64]{0,1:T(8,128)S(1)} all-reduce(f32[64,64]{0,1:T(8,128)S(1)} %convolution_bitcast_fusion), channel_id=1, replica_groups=mesh['row'=8,'col'=16] {'row'}, use_global_device_ids=true, to_apply=%region_14.15 | all-reduce | flops 4096 | bytes 32768 | tf_op jit(solution)/shard_map/psum | solution.py:46
  803.0 0.6 fusion
  803.6 0.7 dynamic-slice_select_fusion
  804.3 56.4 %all-reduce.23.cloned.1.call-done = f32[64,1024]{1,0:T(8,128)} async-done(((f32[64,1024]{1,0:T(8,128)}), f32[64,1024]{1,0:T(8,128)}) %all-reduce.23.cloned.1.call-update) | async-done | bytes 262160 | tf_op jit(solution)/shard_map/psum | solution.py:9
  860.7 11.2 %convolution_subtract_fusion = f32[2048,1024]{1,0:T(8,128)} fusion(f32[2048,1024]{1,0:T(8,128)} %copy-done.2, f32[64,2048]{1,0:T(8,128)S(1)} %fusion, f32[64,2048]{1,0:T(8,128)S(1)} %bitcast.90, f32[64,1024]{1,0:T(8,128)S(1)} %copy-done.5, f32[64,1024]{1,0:T(8,128)} %all-reduce.23.cloned.1.call-done), kind=kOutput, calls=%fused_computation | convolution fusion | flops 3223715840 | bytes 18350080 | tf_op jit(solution)/shard_map/dot_general | solution.py:56
  (36 shorter events, 2.5 us)
Async XLA Ops:
  6.5 183.3 %copy-start.7 = (f32[4,64,64]{2,1,0:T(8,128)S(1)}, f32[4,64,64]{2,1,0:T(8,128)}, u32[]{:S(2)}) copy-start(f32[4,64,64]{2,1,0:T(8,128)} %param.5) | copy-start | bytes 196612
  6.5 86.9 %all-reduce.13.cloned.1.call-start = ((), (), s32[]{:S(2)}) async-start(), calls=%async_computation | async-start | bytes 524288 | tf_op jit(solution)/shard_map/psum | solution.py:9
  33.4 156.5 %all-reduce.15.cloned.1.call-start = ((), (), s32[]{:S(2)}) async-start(), calls=%async_computation.1 | async-start | bytes 1048576 | tf_op jit(solution)/shard_map/psum | solution.py:35
  93.4 182.2 %copy-start.6 = (f32[64,1024]{1,0:T(8,128)S(1)}, f32[64,1024]{1,0:T(8,128)}, u32[]{:S(2)}) copy-start(f32[64,1024]{1,0:T(8,128)} %all-reduce.13.cloned.1.call-done) | copy-start | bytes 786436
  105.7 169.9 %all-reduce.29.cloned.1.call-start = ((), (), s32[]{:S(2)}) async-start(), calls=%async_computation.8 | async-start | bytes 1048576 | tf_op jit(solution)/shard_map/psum | solution.py:9
  218.1 167.2 %all-reduce.17.cloned.1.call-start = ((), (), s32[]{:S(2)}) async-start(), calls=%async_computation.2 | async-start | bytes 1048576 | tf_op jit(solution)/shard_map/psum | solution.py:35
  275.6 16.3 %copy-start.4 = (f32[64,1024]{1,0:T(8,128)S(1)}, f32[64,1024]{1,0:T(8,128)}, u32[]{:S(2)}) copy-start(f32[64,1024]{1,0:T(8,128)} %get-tuple-element.10) | copy-start | bytes 786436
  288.4 3.4 copy-start.1
  300.8 170.2 %all-reduce.27.cloned.1.call-start = ((), (), s32[]{:S(2)}) async-start(), calls=%async_computation.7 | async-start | bytes 1048576 | tf_op jit(solution)/shard_map/psum | solution.py:9
  413.4 167.3 %all-reduce.19.cloned.1.call-start = ((), (), s32[]{:S(2)}) async-start(), calls=%async_computation.3 | async-start | bytes 1048576 | tf_op jit(solution)/shard_map/psum | solution.py:35
  471.0 16.3 %copy-start.3 = (f32[64,1024]{1,0:T(8,128)S(1)}, f32[64,1024]{1,0:T(8,128)}, u32[]{:S(2)}) copy-start(f32[64,1024]{1,0:T(8,128)} %get-tuple-element.8) | copy-start | bytes 786436
  483.9 3.4 copy-start
  496.2 170.1 %all-reduce.25.cloned.1.call-start = ((), (), s32[]{:S(2)}) async-start(), calls=%async_computation.6 | async-start | bytes 1048576 | tf_op jit(solution)/shard_map/psum | solution.py:9
  608.8 167.0 %all-reduce.21.cloned.1.call-start = ((), (), s32[]{:S(2)}) async-start(), calls=%async_computation.4 | async-start | bytes 1048576 | tf_op jit(solution)/shard_map/psum | solution.py:35
  666.3 16.3 %copy-start.5 = (f32[64,1024]{1,0:T(8,128)S(1)}, f32[64,1024]{1,0:T(8,128)}, u32[]{:S(2)}) copy-start(f32[64,1024]{1,0:T(8,128)} %get-tuple-element.6) | copy-start | bytes 786436
  679.2 3.4 copy-start.2
  691.5 169.2 %all-reduce.23.cloned.1.call-start = ((), (), s32[]{:S(2)}) async-start(), calls=%async_computation.5 | async-start | bytes 524288 | tf_op jit(solution)/shard_map/psum | solution.py:9
Sparse Core Ops, SparseCore 0:
  33.5 59.8 all-reduce.12
  105.8 84.0 all-reduce.14
  218.2 57.3 all-reduce.28
  300.9 84.2 all-reduce.16
  413.5 57.4 all-reduce.26
  496.3 84.2 all-reduce.18
  608.9 57.3 all-reduce.24
  691.6 84.1 all-reduce.20
  804.4 56.2 all-reduce.22
where the time goes:
time: 886 us; the launch traced here: 879 us
  waiting for transfers between devices  547 us (62%)
  blocking collectives  199 us (22%)
  matrix products  101 us (11%)
  between operations  13.6 us (2%)
  local copies, waits for them, and re-layouts  11 us (1%)
    psum x5, waiting for transfers between devices, broadcast(): return lax.psum(kept, axis)  288 us
    psum x4, waiting for transfers between devices, shards(): product_rows = lax.psum(partial_value, 'col')  259 us
    all_gather x4, blocking collectives, shards(): reflect_rows = lax.all_gather(piece, 'col', axis=1, tiled=True)  101 us
    psum x4, blocking collectives, shards(): inner = lax.psum(local_inner, 'row')  98.1 us
    dot_general x4, matrix products, shards(): lax.dot_general(left_block, right_block, (((0,), (0,)), ((), ())), precis...  49.8 us
    dot_general x4, matrix products, shards(): lax.dot_general(reflect_cols, matrix, (((1,), (1,)), ((), ())), precision...  39 us
  transfers between devices with their start and end apart: 9, of which 9 were waited for; matrix products, arithmetic and copies ran while one was open for 0% of the time, Pallas kernels for 0%

commit v1 on v0

--- a/solution.py
+++ b/solution.py
@@ -1,7 +1,22 @@
+import functools
 import jax
 import jax.numpy as jnp
 from jax import lax
 from jax.sharding import PartitionSpec as P
+from jax.lax import axis_size, ppermute
+
+
+def _unite_turns(vals, a_name):
+    n_peers_all = axis_size(a_name)
+    main = vals
+    for kk in [
+        [(nth, nth ^ p) for nth in range(n_peers_all)] for p in (1, 2, 4, 8, 16) if p < n_peers_all
+    ]:
+        main = main + ppermute(main, axis_name=a_name, perm=kk)
+    return main
+
+
+draw_case_over_axis = functools.partial(_unite_turns, a_name="col")
 
 
 def broadcast(value, axis, source):
@@ -32,7 +47,7 @@
             precision=highest,
             preferred_element_type=jnp.float32,
         )
-        product_rows = lax.psum(partial_value, "col")
+        product_rows = draw_case_over_axis(partial_value)
         image_rows = jnp.dot(
             factor.T, product_rows, precision=highest, preferred_element_type=jnp.float32
         )

time: 886 us -> 817 us (0.922)
  waiting for transfers between devices: 547 us -> 422 us
  starting transfers between devices: 1.09 us -> 39.6 us
  blocking collectives: 199 us -> 225 us
    psum x4 -> x0, waiting for transfers between devices: 259 us -> none  [shards(): product_rows = lax.psum(partial_value, 'col')]
    ppermute x0 -> x16, waiting for transfers between devices: none -> 129 us  [_unite_turns(): main = main + ppermute(main, axis_name=a_name, perm=kk)]
    ppermute x0 -> x16, starting transfers between devices: none -> 39.3 us  [_unite_turns(): main = main + ppermute(main, axis_name=a_name, perm=kk)]
    psum x4, blocking collectives: 98.1 us -> 118 us  [shards(): inner = lax.psum(local_inner, 'row')]
  transfers between devices with their start and end apart: 9 -> 21, of which waited for: 9 -> 18; matrix products, arithmetic and copies ran while one was open for 0% -> 0% of each run, Pallas kernels for 0% -> 0%
where the time goes in v1:
time: 817 us; the launch traced here: 811 us
  waiting for transfers between devices  422 us (52%)
  blocking collectives  225 us (28%)
  matrix products  93.3 us (11%)
  starting transfers between devices  39.6 us (5%)
  between operations  13.6 us (2%)
  local copies, waits for them, and re-layouts  11 us (1%)
    psum x5, waiting for transfers between devices, broadcast(): return lax.psum(kept, axis)  293 us
    ppermute x16, waiting for transfers between devices, _unite_turns(): main = main + ppermute(main, axis_name=a_name, perm=kk)  129 us
    psum x4, blocking collectives, shards(): inner = lax.psum(local_inner, 'row')  118 us
    all_gather x4, blocking collectives, shards(): reflect_rows = lax.all_gather(piece, 'col', axis=1, tiled=True)  107 us
    dot_general x4, matrix products, shards(): lax.dot_general(left_block, right_block, (((0,), (0,)), ((), ())), precis...  49.8 us
    ppermute x16, starting transfers between devices, _unite_turns(): main = main + ppermute(main, axis_name=a_name, perm=kk)  39.3 us
    dot_general x4, matrix products, shards(): lax.dot_general(reflect_cols, matrix, (((1,), (1,)), ((), ())), precision...  35.7 us
  transfers between devices with their start and end apart: 21, of which 18 were waited for; matrix products, arithmetic and copies ran while one was open for 0% of the time, Pallas kernels for 0%

profile of v1, /device:TPU:0, one launch (start us, length us, event | category | flops | bytes accessed | tf_op | source)
XLA Modules:
  0.0 811.3 jit_solution(6296724533998869244)
XLA Ops:
  7.4 25.2 %all-gather = f32[1,64,2048]{2,1,0:T(8,128)S(1)} all-gather(f32[1,64,128]{2,1,0:T(8,128)S(1)} %get-tuple-element.13), channel_id=2, replica_groups=mesh['row'=8,'col'=16] {'col'}, dimensions={2}, use_global_device_ids=true | all-gather | bytes 557056 | tf_op jit(solution)/shard_map/all_gather | solution.py:39
  33.4 60.0 %all-reduce.9.cloned.1.call-done = f32[64,1024]{1,0:T(8,128)} async-done(((f32[64,1024]{1,0:T(8,128)}), f32[64,1024]{1,0:T(8,128)}) %all-reduce.9.cloned.1.call-update) | async-done | bytes 262160 | tf_op jit(solution)/shard_map/psum | solution.py:24
  93.4 11.4 %fusion.65 = f32[64,2048]{1,0:T(8,128)S(1)} fusion(f32[64,1024]{1,0:T(8,128)} %all-reduce.9.cloned.1.call-done, f32[2048,1024]{1,0:T(8,128)} %param.3), kind=kOutput, calls=%fused_computation.89 | convolution fusion | flops 1610612736 | bytes 9175040 | tf_op jit(solution)/shard_map/dot_general | solution.py:43
  106.4 10.1 %collective-permute-done = f32[64,2048]{1,0:T(8,128)S(1)} collective-permute-done((f32[64,2048]{1,0:T(8,128)S(1)}, f32[64,2048]{1,0:T(8,128)S(1)}, u32[]{:S(2)}, u32[]{:S(2)}) %collective-permute-start) | collective-permute-done | bytes 524320 | tf_op jit(solution)/shard_map/ppermute | solution.py:15
  116.5 3.1 collective-permute-start.1
  119.6 10.2 %collective-permute-done.1 = f32[64,2048]{1,0:T(8,128)S(1)} collective-permute-done((f32[64,2048]{1,0:T(8,128)S(1)}, f32[64,2048]{1,0:T(8,128)S(1)}, u32[]{:S(2)}, u32[]{:S(2)}) %collective-permute-start.1) | collective-permute-done | bytes 524320 | tf_op jit(solution)/shard_map/ppermute | solution.py:15
  129.9 1.6 collective-permute-start.2
  131.5 9.3 %collective-permute-done.2 = f32[64,2048]{1,0:T(8,128)S(1)} collective-permute-done((f32[64,2048]{1,0:T(8,128)S(1)}, f32[64,2048]{1,0:T(8,128)S(1)}, u32[]{:S(2)}, u32[]{:S(2)}) %collective-permute-start.2) | collective-permute-done | bytes 524320 | tf_op jit(solution)/shard_map/ppermute | solution.py:15
  140.9 3.6 collective-permute-start.3
  144.5 27.4 %all-gather.1 = f32[1,64,2048]{2,1,0:T(8,128)S(1)} all-gather(f32[1,64,128]{2,1,0:T(8,128)S(1)} %get-tuple-element.12), channel_id=3, replica_groups=mesh['row'=8,'col'=16] {'col'}, dimensions={2}, use_global_device_ids=true | all-gather | bytes 557056 | tf_op jit(solution)/shard_map/all_gather | solution.py:39
  173.8 29.2 %psum.85 = f32[64,64]{0,1:T(8,128)S(1)} all-reduce(f32[64,64]{0,1:T(8,128)S(1)} %convolution_bitcast_fusion.3), channel_id=1, replica_groups=mesh['row'=8,'col'=16] {'row'}, use_global_device_ids=true, to_apply=%region_1.2 | all-reduce | flops 4096 | bytes 32768 | tf_op jit(solution)/shard_map/psum | solution.py:61
  204.8 58.1 %all-reduce.17.cloned.1.call-done = (f32[64,1024]{1,0:T(8,128)}, f32[64,1024]{1,0:T(8,128)}) async-done(((f32[64,1024]{1,0:T(8,128)}, f32[64,1024]{1,0:T(8,128)}), (f32[64,1024]{1,0:T(8,128)}, f32[64,1024]{1,0:T(8,128)})) %all-reduce.17.cloned.1.call-update) | async-done | bytes 524304 | tf_op jit(solution)/shard_map/psum | solution.py:24
  262.8 12.9 %convolution_subtract_fusion.3 = f32[2048,1024]{1,0:T(8,128)S(1)} fusion(f32[2048,1024]{1,0:T(8,128)} %param.3, f32[64,2048]{1,0:T(8,128)S(1)} %bitcast_subtract_fusion.3, f32[64,2048]{1,0:T(8,128)S(1)} %bitcast.87, f32[64,1024]{1,0:T(8,128)S(1)} %copy-done.6, f32[64,1024]{1,0:T(8,128)} %get-tuple-element.9), kind=kOutput, calls=%fused_computation.3 | convolution fusion | flops 3223715840 | bytes 18350080 | tf_op jit(solution)/shard_map/dot_general | solution.py:71
  275.7 3.4 copy-done.1
  279.1 8.1 fusion.66
  288.8 10.2 %collective-permute-done.4 = f32[64,2048]{1,0:T(8,128)S(1)} collective-permute-done((f32[64,2048]{1,0:T(8,128)S(1)}, f32[64,2048]{1,0:T(8,128)S(1)}, u32[]{:S(2)}, u32[]{:S(2)}) %collective-permute-start.4) | collective-permute-done | bytes 524320 | tf_op jit(solution)/shard_map/ppermute | solution.py:15
  299.1 3.1 collective-permute-start.5
  302.1 10.2 %collective-permute-done.5 = f32[64,2048]{1,0:T(8,128)S(1)} collective-permute-done((f32[64,2048]{1,0:T(8,128)S(1)}, f32[64,2048]{1,0:T(8,128)S(1)}, u32[]{:S(2)}, u32[]{:S(2)}) %collective-permute-start.5) | collective-permute-done | bytes 524320 | tf_op jit(solution)/shard_map/ppermute | solution.py:15
  312.4 1.6 collective-permute-start.6
  314.0 9.3 %collective-permute-done.6 = f32[64,2048]{1,0:T(8,128)S(1)} collective-permute-done((f32[64,2048]{1,0:T(8,128)S(1)}, f32[64,2048]{1,0:T(8,128)S(1)}, u32[]{:S(2)}, u32[]{:S(2)}) %collective-permute-start.6) | collective-permute-done | bytes 524320 | tf_op jit(solution)/shard_map/ppermute | solution.py:15
  323.4 3.6 collective-permute-start.7
  327.0 27.4 %all-gather.2 = f32[1,64,2048]{2,1,0:T(8,128)S(1)} all-gather(f32[1,64,128]{2,1,0:T(8,128)S(1)} %get-tuple-element.14), channel_id=4, replica_groups=mesh['row'=8,'col'=16] {'col'}, dimensions={2}, use_global_device_ids=true | all-gather | bytes 557056 | tf_op jit(solution)/shard_map/all_gather | solution.py:39
  356.3 29.8 %psum.88 = f32[64,64]{0,1:T(8,128)S(1)} all-reduce(f32[64,64]{0,1:T(8,128)S(1)} %convolution_bitcast_fusion.2), channel_id=1, replica_groups=mesh['row'=8,'col'=16] {'row'}, use_global_device_ids=true, to_apply=%region_4.5 | all-reduce | flops 4096 | bytes 32768 | tf_op jit(solution)/shard_map/psum | solution.py:61
  387.6 58.2 %all-reduce.15.cloned.1.call-done = (f32[64,1024]{1,0:T(8,128)}, f32[64,1024]{1,0:T(8,128)}) async-done(((f32[64,1024]{1,0:T(8,128)}, f32[64,1024]{1,0:T(8,128)}), (f32[64,1024]{1,0:T(8,128)}, f32[64,1024]{1,0:T(8,128)})) %all-reduce.15.cloned.1.call-update) | async-done | bytes 524304 | tf_op jit(solution)/shard_map/psum | solution.py:24
  445.8 12.9 %convolution_subtract_fusion.2 = f32[2048,1024]{1,0:T(8,128)S(1)} fusion(f32[2048,1024]{1,0:T(8,128)} %copy-done.1, f32[64,2048]{1,0:T(8,128)S(1)} %bitcast_subtract_fusion.2, f32[64,2048]{1,0:T(8,128)S(1)} %bitcast.85, f32[64,1024]{1,0:T(8,128)S(1)} %copy-done.4, f32[64,1024]{1,0:T(8,128)} %get-tuple-element.7), kind=kOutput, calls=%fused_computation.2 | convolution fusion | flops 3223715840 | bytes 18350080 | tf_op jit(solution)/shard_map/dot_general | solution.py:71
  458.7 3.4 copy-done
  462.1 8.1 fusion.67
  471.8 10.2 %collective-permute-done.8 = f32[64,2048]{1,0:T(8,128)S(1)} collective-permute-done((f32[64,2048]{1,0:T(8,128)S(1)}, f32[64,2048]{1,0:T(8,128)S(1)}, u32[]{:S(2)}, u32[]{:S(2)}) %collective-permute-start.8) | collective-permute-done | bytes 524320 | tf_op jit(solution)/shard_map/ppermute | solution.py:15
  482.1 3.1 collective-permute-start.9
  485.1 10.2 %collective-permute-done.9 = f32[64,2048]{1,0:T(8,128)S(1)} collective-permute-done((f32[64,2048]{1,0:T(8,128)S(1)}, f32[64,2048]{1,0:T(8,128)S(1)}, u32[]{:S(2)}, u32[]{:S(2)}) %collective-permute-start.9) | collective-permute-done | bytes 524320 | tf_op jit(solution)/shard_map/ppermute | solution.py:15
  495.5 1.6 collective-permute-start.10
  497.0 9.3 %collective-permute-done.10 = f32[64,2048]{1,0:T(8,128)S(1)} collective-permute-done((f32[64,2048]{1,0:T(8,128)S(1)}, f32[64,2048]{1,0:T(8,128)S(1)}, u32[]{:S(2)}, u32[]{:S(2)}) %collective-permute-start.10) | collective-permute-done | bytes 524320 | tf_op jit(solution)/shard_map/ppermute | solution.py:15
  506.4 3.6 collective-permute-start.11
  510.1 27.4 %all-gather.3 = f32[1,64,2048]{2,1,0:T(8,128)S(1)} all-gather(f32[1,64,128]{2,1,0:T(8,128)S(1)} %get-tuple-element.11), channel_id=5, replica_groups=mesh['row'=8,'col'=16] {'col'}, dimensions={2}, use_global_device_ids=true | all-gather | bytes 557056 | tf_op jit(solution)/shard_map/all_gather | solution.py:39
  539.3 29.8 %psum.91 = f32[64,64]{0,1:T(8,128)S(1)} all-reduce(f32[64,64]{0,1:T(8,128)S(1)} %convolution_bitcast_fusion.1), channel_id=1, replica_groups=mesh['row'=8,'col'=16] {'row'}, use_global_device_ids=true, to_apply=%region_7.8 | all-reduce | flops 4096 | bytes 32768 | tf_op jit(solution)/shard_map/psum | solution.py:61
  570.7 58.2 %all-reduce.13.cloned.1.call-done = (f32[64,1024]{1,0:T(8,128)}, f32[64,1024]{1,0:T(8,128)}) async-done(((f32[64,1024]{1,0:T(8,128)}, f32[64,1024]{1,0:T(8,128)}), (f32[64,1024]{1,0:T(8,128)}, f32[64,1024]{1,0:T(8,128)})) %all-reduce.13.cloned.1.call-update) | async-done | bytes 524304 | tf_op jit(solution)/shard_map/psum | solution.py:24
  628.9 12.9 %convolution_subtract_fusion.1 = f32[2048,1024]{1,0:T(8,128)S(1)} fusion(f32[2048,1024]{1,0:T(8,128)} %copy-done, f32[64,2048]{1,0:T(8,128)S(1)} %bitcast_subtract_fusion.1, f32[64,2048]{1,0:T(8,128)S(1)} %bitcast.84, f32[64,1024]{1,0:T(8,128)S(1)} %copy-done.3, f32[64,1024]{1,0:T(8,128)} %get-tuple-element.5), kind=kOutput, calls=%fused_computation.1 | convolution fusion | flops 3223715840 | bytes 18350080 | tf_op jit(solution)/shard_map/dot_general | solution.py:71
  641.8 3.4 copy-done.2
  645.2 8.1 fusion.68
  654.8 10.2 %collective-permute-done.12 = f32[64,2048]{1,0:T(8,128)S(1)} collective-permute-done((f32[64,2048]{1,0:T(8,128)S(1)}, f32[64,2048]{1,0:T(8,128)S(1)}, u32[]{:S(2)}, u32[]{:S(2)}) %collective-permute-start.12) | collective-permute-done | bytes 524320 | tf_op jit(solution)/shard_map/ppermute | solution.py:15
  665.1 3.1 collective-permute-start.13
  668.2 10.2 %collective-permute-done.13 = f32[64,2048]{1,0:T(8,128)S(1)} collective-permute-done((f32[64,2048]{1,0:T(8,128)S(1)}, f32[64,2048]{1,0:T(8,128)S(1)}, u32[]{:S(2)}, u32[]{:S(2)}) %collective-permute-start.13) | collective-permute-done | bytes 524320 | tf_op jit(solution)/shard_map/ppermute | solution.py:15
  680.1 9.3 %collective-permute-done.14 = f32[64,2048]{1,0:T(8,128)S(1)} collective-permute-done((f32[64,2048]{1,0:T(8,128)S(1)}, f32[64,2048]{1,0:T(8,128)S(1)}, u32[]{:S(2)}, u32[]{:S(2)}) %collective-permute-start.14) | collective-permute-done | bytes 524320 | tf_op jit(solution)/shard_map/ppermute | solution.py:15
  689.4 3.6 collective-permute-start.15
  693.1 9.7 %collective-permute-done.15 = f32[64,2048]{1,0:T(8,128)S(1)} collective-permute-done((f32[64,2048]{1,0:T(8,128)S(1)}, f32[64,2048]{1,0:T(8,128)S(1)}, u32[]{:S(2)}, u32[]{:S(2)}) %collective-permute-start.15) | collective-permute-done | bytes 524320 | tf_op jit(solution)/shard_map/ppermute | solution.py:15
  704.0 29.0 %psum.94 = f32[64,64]{0,1:T(8,128)S(1)} all-reduce(f32[64,64]{0,1:T(8,128)S(1)} %convolution_bitcast_fusion), channel_id=1, replica_groups=mesh['row'=8,'col'=16] {'row'}, use_global_device_ids=true, to_apply=%region_10.11 | all-reduce | flops 4096 | bytes 32768 | tf_op jit(solution)/shard_map/psum | solution.py:61
  734.5 58.9 %all-reduce.11.cloned.1.call-done = f32[64,1024]{1,0:T(8,128)} async-done(((f32[64,1024]{1,0:T(8,128)}), f32[64,1024]{1,0:T(8,128)}) %all-reduce.11.cloned.1.call-update) | async-done | bytes 262160 | tf_op jit(solution)/shard_map/psum | solution.py:24
  793.4 11.2 %convolution_subtract_fusion = f32[2048,1024]{1,0:T(8,128)} fusion(f32[2048,1024]{1,0:T(8,128)} %copy-done.2, f32[64,2048]{1,0:T(8,128)S(1)} %bitcast_subtract_fusion, f32[64,2048]{1,0:T(8,128)S(1)} %bitcast.86, f32[64,1024]{1,0:T(8,128)S(1)} %copy-done.5, f32[64,1024]{1,0:T(8,128)} %all-reduce.11.cloned.1.call-done), kind=kOutput, calls=%fused_computation | convolution fusion | flops 3223715840 | bytes 18350080 | tf_op jit(solution)/shard_map/dot_general | solution.py:71
  (68 shorter events, 23.3 us)
Async XLA Ops:
  6.5 166.1 %copy-start.7 = (f32[4,64,64]{2,1,0:T(8,128)S(1)}, f32[4,64,64]{2,1,0:T(8,128)}, u32[]{:S(2)}) copy-start(f32[4,64,64]{2,1,0:T(8,128)} %param.5) | copy-start | bytes 196612
  6.5 86.9 %all-reduce.9.cloned.1.call-start = ((), (), s32[]{:S(2)}) async-start(), calls=%async_computation | async-start | bytes 524288 | tf_op jit(solution)/shard_map/psum | solution.py:24
  33.4 229.5 %all-reduce.17.cloned.1.call-start = ((), (), s32[]{:S(2)}) async-start(), calls=%async_computation.4 | async-start | bytes 1048576 | tf_op jit(solution)/shard_map/psum | solution.py:24
  93.4 169.4 %copy-start.6 = (f32[64,1024]{1,0:T(8,128)S(1)}, f32[64,1024]{1,0:T(8,128)}, u32[]{:S(2)}) copy-start(f32[64,1024]{1,0:T(8,128)} %all-reduce.9.cloned.1.call-done) | copy-start | bytes 786436
  104.8 11.7 %collective-permute-start = (f32[64,2048]{1,0:T(8,128)S(1)}, f32[64,2048]{1,0:T(8,128)S(1)}, u32[]{:S(2)}, u32[]{:S(2)}) collective-permute-start(f32[64,2048]{1,0:T(8,128)S(1)} %fusion.65), channel_id=1, source_target_pairs={{0,1},{1,0},{2,3},{3,2},{4,5},{5,4},{6,7},{7,6},{8,9},{9,8},{10,11... | collective-permute-start | bytes 1572872 | tf_op jit(solution)/shard_map/ppermute | solution.py:15
  116.5 13.3 %collective-permute-start.1 = (f32[64,2048]{1,0:T(8,128)S(1)}, f32[64,2048]{1,0:T(8,128)S(1)}, u32[]{:S(2)}, u32[]{:S(2)}) collective-permute-start(f32[64,2048]{1,0:T(8,128)S(1)} %add.89), channel_id=1, source_target_pairs={{0,2},{1,3},{2,0},{3,1},{4,6},{5,7},{6,4},{7,5},{8,10},{9,11},{10,... | collective-permute-start | bytes 1572872 | tf_op jit(solution)/shard_map/ppermute | solution.py:15
  129.9 10.9 %collective-permute-start.2 = (f32[64,2048]{1,0:T(8,128)S(1)}, f32[64,2048]{1,0:T(8,128)S(1)}, u32[]{:S(2)}, u32[]{:S(2)}) collective-permute-start(f32[64,2048]{1,0:T(8,128)S(1)} %add.90), channel_id=1, source_target_pairs={{0,4},{1,5},{2,6},{3,7},{4,0},{5,1},{6,2},{7,3},{8,12},{9,13},{10,... | collective-permute-start | bytes 1572872 | tf_op jit(solution)/shard_map/ppermute | solution.py:15
  140.9 31.8 %collective-permute-start.3 = (f32[64,2048]{1,0:T(8,128)S(1)}, f32[64,2048]{1,0:T(8,128)S(1)}, u32[]{:S(2)}, u32[]{:S(2)}) collective-permute-start(f32[64,2048]{1,0:T(8,128)S(1)} %add.91), channel_id=1, source_target_pairs={{0,8},{1,9},{2,10},{3,11},{4,12},{5,13},{6,14},{7,15},{8,0},{9,1},... | collective-permute-start | bytes 1572872 | tf_op jit(solution)/shard_map/ppermute | solution.py:15
  204.5 241.3 %all-reduce.15.cloned.1.call-start = ((), (), s32[]{:S(2)}) async-start(), calls=%async_computation.3 | async-start | bytes 1048576 | tf_op jit(solution)/shard_map/psum | solution.py:24
  262.8 16.3 %copy-start.4 = (f32[64,1024]{1,0:T(8,128)S(1)}, f32[64,1024]{1,0:T(8,128)}, u32[]{:S(2)}) copy-start(f32[64,1024]{1,0:T(8,128)} %get-tuple-element.10) | copy-start | bytes 786436
  275.7 3.4 copy-start.1
  287.2 11.8 %collective-permute-start.4 = (f32[64,2048]{1,0:T(8,128)S(1)}, f32[64,2048]{1,0:T(8,128)S(1)}, u32[]{:S(2)}, u32[]{:S(2)}) collective-permute-start(f32[64,2048]{1,0:T(8,128)S(1)} %fusion.66), channel_id=1, source_target_pairs={{0,1},{1,0},{2,3},{3,2},{4,5},{5,4},{6,7},{7,6},{8,9},{9,8},{10,11... | collective-permute-start | bytes 1572872 | tf_op jit(solution)/shard_map/ppermute | solution.py:15
  299.1 13.3 %collective-permute-start.5 = (f32[64,2048]{1,0:T(8,128)S(1)}, f32[64,2048]{1,0:T(8,128)S(1)}, u32[]{:S(2)}, u32[]{:S(2)}) collective-permute-start(f32[64,2048]{1,0:T(8,128)S(1)} %add.93), channel_id=1, source_target_pairs={{0,2},{1,3},{2,0},{3,1},{4,6},{5,7},{6,4},{7,5},{8,10},{9,11},{10,... | collective-permute-start | bytes 1572872 | tf_op jit(solution)/shard_map/ppermute | solution.py:15
  312.4 10.9 %collective-permute-start.6 = (f32[64,2048]{1,0:T(8,128)S(1)}, f32[64,2048]{1,0:T(8,128)S(1)}, u32[]{:S(2)}, u32[]{:S(2)}) collective-permute-start(f32[64,2048]{1,0:T(8,128)S(1)} %add.94), channel_id=1, source_target_pairs={{0,4},{1,5},{2,6},{3,7},{4,0},{5,1},{6,2},{7,3},{8,12},{9,13},{10,... | collective-permute-start | bytes 1572872 | tf_op jit(solution)/shard_map/ppermute | solution.py:15
  323.4 31.7 %collective-permute-start.7 = (f32[64,2048]{1,0:T(8,128)S(1)}, f32[64,2048]{1,0:T(8,128)S(1)}, u32[]{:S(2)}, u32[]{:S(2)}) collective-permute-start(f32[64,2048]{1,0:T(8,128)S(1)} %add.95), channel_id=1, source_target_pairs={{0,8},{1,9},{2,10},{3,11},{4,12},{5,13},{6,14},{7,15},{8,0},{9,1},... | collective-permute-start | bytes 1572872 | tf_op jit(solution)/shard_map/ppermute | solution.py:15
  387.6 241.3 %all-reduce.13.cloned.1.call-start = ((), (), s32[]{:S(2)}) async-start(), calls=%async_computation.2 | async-start | bytes 1048576 | tf_op jit(solution)/shard_map/psum | solution.py:24
  445.8 16.3 %copy-start.3 = (f32[64,1024]{1,0:T(8,128)S(1)}, f32[64,1024]{1,0:T(8,128)}, u32[]{:S(2)}) copy-start(f32[64,1024]{1,0:T(8,128)} %get-tuple-element.8) | copy-start | bytes 786436
  458.7 3.4 copy-start
  470.2 11.8 %collective-permute-start.8 = (f32[64,2048]{1,0:T(8,128)S(1)}, f32[64,2048]{1,0:T(8,128)S(1)}, u32[]{:S(2)}, u32[]{:S(2)}) collective-permute-start(f32[64,2048]{1,0:T(8,128)S(1)} %fusion.67), channel_id=1, source_target_pairs={{0,1},{1,0},{2,3},{3,2},{4,5},{5,4},{6,7},{7,6},{8,9},{9,8},{10,11... | collective-permute-start | bytes 1572872 | tf_op jit(solution)/shard_map/ppermute | solution.py:15
  482.1 13.3 %collective-permute-start.9 = (f32[64,2048]{1,0:T(8,128)S(1)}, f32[64,2048]{1,0:T(8,128)S(1)}, u32[]{:S(2)}, u32[]{:S(2)}) collective-permute-start(f32[64,2048]{1,0:T(8,128)S(1)} %add.97), channel_id=1, source_target_pairs={{0,2},{1,3},{2,0},{3,1},{4,6},{5,7},{6,4},{7,5},{8,10},{9,11},{10,... | collective-permute-start | bytes 1572872 | tf_op jit(solution)/shard_map/ppermute | solution.py:15
  495.5 10.9 %collective-permute-start.10 = (f32[64,2048]{1,0:T(8,128)S(1)}, f32[64,2048]{1,0:T(8,128)S(1)}, u32[]{:S(2)}, u32[]{:S(2)}) collective-permute-start(f32[64,2048]{1,0:T(8,128)S(1)} %add.98), channel_id=1, source_target_pairs={{0,4},{1,5},{2,6},{3,7},{4,0},{5,1},{6,2},{7,3},{8,12},{9,13},{10,... | collective-permute-start | bytes 1572872 | tf_op jit(solution)/shard_map/ppermute | solution.py:15
  506.4 31.7 %collective-permute-start.11 = (f32[64,2048]{1,0:T(8,128)S(1)}, f32[64,2048]{1,0:T(8,128)S(1)}, u32[]{:S(2)}, u32[]{:S(2)}) collective-permute-start(f32[64,2048]{1,0:T(8,128)S(1)} %add.99), channel_id=1, source_target_pairs={{0,8},{1,9},{2,10},{3,11},{4,12},{5,13},{6,14},{7,15},{8,0},{9,1},... | collective-permute-start | bytes 1572872 | tf_op jit(solution)/shard_map/ppermute | solution.py:15
  570.6 222.7 %all-reduce.11.cloned.1.call-start = ((), (), s32[]{:S(2)}) async-start(), calls=%async_computation.1 | async-start | bytes 524288 | tf_op jit(solution)/shard_map/psum | solution.py:24
  628.9 16.3 %copy-start.5 = (f32[64,1024]{1,0:T(8,128)S(1)}, f32[64,1024]{1,0:T(8,128)}, u32[]{:S(2)}) copy-start(f32[64,1024]{1,0:T(8,128)} %get-tuple-element.6) | copy-start | bytes 786436
  641.8 3.4 copy-start.2
  653.3 11.8 %collective-permute-start.12 = (f32[64,2048]{1,0:T(8,128)S(1)}, f32[64,2048]{1,0:T(8,128)S(1)}, u32[]{:S(2)}, u32[]{:S(2)}) collective-permute-start(f32[64,2048]{1,0:T(8,128)S(1)} %fusion.68), channel_id=1, source_target_pairs={{0,1},{1,0},{2,3},{3,2},{4,5},{5,4},{6,7},{7,6},{8,9},{9,8},{10,11... | collective-permute-start | bytes 1572872 | tf_op jit(solution)/shard_map/ppermute | solution.py:15
  665.1 13.3 %collective-permute-start.13 = (f32[64,2048]{1,0:T(8,128)S(1)}, f32[64,2048]{1,0:T(8,128)S(1)}, u32[]{:S(2)}, u32[]{:S(2)}) collective-permute-start(f32[64,2048]{1,0:T(8,128)S(1)} %add.101), channel_id=1, source_target_pairs={{0,2},{1,3},{2,0},{3,1},{4,6},{5,7},{6,4},{7,5},{8,10},{9,11},{10,... | collective-permute-start | bytes 1572872 | tf_op jit(solution)/shard_map/ppermute | solution.py:15
  678.5 10.9 %collective-permute-start.14 = (f32[64,2048]{1,0:T(8,128)S(1)}, f32[64,2048]{1,0:T(8,128)S(1)}, u32[]{:S(2)}, u32[]{:S(2)}) collective-permute-start(f32[64,2048]{1,0:T(8,128)S(1)} %add.102), channel_id=1, source_target_pairs={{0,4},{1,5},{2,6},{3,7},{4,0},{5,1},{6,2},{7,3},{8,12},{9,13},{10,... | collective-permute-start | bytes 1572872 | tf_op jit(solution)/shard_map/ppermute | solution.py:15
  689.4 13.3 %collective-permute-start.15 = (f32[64,2048]{1,0:T(8,128)S(1)}, f32[64,2048]{1,0:T(8,128)S(1)}, u32[]{:S(2)}, u32[]{:S(2)}) collective-permute-start(f32[64,2048]{1,0:T(8,128)S(1)} %add.103), channel_id=1, source_target_pairs={{0,8},{1,9},{2,10},{3,11},{4,12},{5,13},{6,14},{7,15},{8,0},{9,1},... | collective-permute-start | bytes 1572872 | tf_op jit(solution)/shard_map/ppermute | solution.py:15
Sparse Core Ops, SparseCore 0:
  33.5 59.8 all-reduce.8
  204.7 58.1 all-reduce.16
  387.7 58.0 all-reduce.14
  570.7 58.0 all-reduce.12
  734.6 58.7 all-reduce.10
